TPU v7x, 128 devices: a whole 4x4x4 slice. The times are simulated.
128 devices in a mesh: req: 32 (over y, x, core), kv: 4 (over z).
Axes of the slice: x: 4, y: 4, z: 4, core: 2. Of those that a mesh axis runs over, the one named last changes fastest.
Arguments:
- tokens: bfloat16 [4096, 2048], P('req'), may hold values from -6 to 6
- lengths: int32 [4096], replicated, may hold values from 1 to 1024, as said below
- page_table: int32 [4096, 16], P('req'), may hold values from 0 to 367, as said below
- key_cache: bfloat16 [11776, 4, 64, 128], P('req', 'kv'), may hold values from -320 to 320
- value_page_cache: bfloat16 [11776, 4, 64, 128], P('req', 'kv'), may hold values from -6 to 6
- mig_slot: int32 [32, 2], replicated, may hold values from 0 to 127, as said below
- attn_gain: float32 [2048], replicated, may hold values from 0.1 to 1.9
- w_query: bfloat16 [2048, 4096], P(None, 'kv'), may hold values from -0.125 to 0.125
- key_weight: bfloat16 [2048, 512], P(None, 'kv'), may hold values from -0.125 to 0.125
- value_weight: bfloat16 [2048, 512], P(None, 'kv'), may hold values from -0.125 to 0.125
- w_out: bfloat16 [4096, 2048], P('kv'), may hold values from -0.09375 to 0.09375
- moe_gain: float32 [2048], replicated, may hold values from 0.1 to 1.9
- routes: int32 [4096, 8], P(('req', 'kv')), may hold values from 0 to 127, all different within a row; in each aligned block of 32 rows (0 to 31, 32 to 63, ...) at most 4 rows name the same one
- gate_probs: float32 [4096, 8], P(('req', 'kv')), may hold values from 0.05 to 1
- w_gate: bfloat16 [128, 2048, 768], P(('req', 'kv')), may hold values from -0.125 to 0.125
- w_up: bfloat16 [128, 2048, 768], P(('req', 'kv')), may hold values from -0.125 to 0.125
- w_down: bfloat16 [128, 768, 2048], P(('req', 'kv')), may hold values from -0.21875 to 0.21875
Outputs:
- layer_out: bfloat16 [4096, 2048], P(('req', 'kv'))
- moved_keys: bfloat16 [64, 4, 1024, 128], P('req', 'kv')
- moved_values: bfloat16 [64, 4, 1024, 128], P('req', 'kv')
Inputs may be any that keep to these rules, and one draw needn't show every extreme that they name: `lengths`: in each block of 128 requests of one index of req, between 2 and 16 requests are longer than 64 tokens and the others are at most 64 long; some request is exactly 1024 long. `page_table`: entries j below the ceiling of lengths[r] / 64 name distinct pages of the pool of request r's own index of req, counted within that pool; later entries are arbitrary pages of that pool. `mig_slot`: row g names 2 distinct local rows of index g of req, each a request longer than 64 tokens. `routes`: in the rows of one device (aligned blocks of 32 rows) no expert is named by more than 4 rows.
All inputs are finite; a program needn't handle non-finite values.
Results may differ from a plain program's by a relative error of at most 0.011.
Values may be sent and summed in bfloat16 or wider, within the bound.
No kernel may reach another device: no remote copies, remote signals or barrier semaphores. Data moves between devices by JAX's collectives and lax.ppermute only.
A program may use at most 128 MiB of HBM per device.

v0:
```python
import math
import jax
import jax.numpy as jnp
from jax import lax
from jax.sharding import PartitionSpec as P

EPSILON = 1e-06
THETA = 1000000.0


def from_behind(shard, axis, by):
    size = lax.axis_size(axis)
    return lax.ppermute(shard, axis, [(i, (i + by) % size) for i in range(size)])


def rms_scale(inputs, gain_vec):
    return (
        inputs * lax.rsqrt(jnp.mean(inputs * inputs, axis=-1, keepdims=True) + EPSILON) * gain_vec
    )


def rotate(vectors, positions):
    half_width = vectors.shape[-1] // 2
    exponent = jnp.arange(half_width, dtype=jnp.float32) * (-2.0 / vectors.shape[-1])
    angles = positions.astype(jnp.float32)[..., None] * THETA**exponent
    cosine = jnp.cos(angles)
    sine_part = jnp.sin(angles)
    front_half = vectors[..., :half_width]
    back_half = vectors[..., half_width:]
    return jnp.concatenate(
        [front_half * cosine - back_half * sine_part, back_half * cosine + front_half * sine_part],
        axis=-1,
    )


def project(token_rows, attn_gain, w_query, key_weight, value_weight, positions):
    normalized_rows = rms_scale(token_rows.astype(jnp.float32), attn_gain).astype(jnp.bfloat16)
    head_size = key_weight.shape[1]
    queries = jnp.dot(normalized_rows, w_query, preferred_element_type=jnp.float32).reshape(
        token_rows.shape[0], -1, head_size
    )
    fresh_key = jnp.dot(normalized_rows, key_weight, preferred_element_type=jnp.float32)
    fresh_value = jnp.dot(normalized_rows, value_weight, preferred_element_type=jnp.float32).astype(
        jnp.bfloat16
    )
    queries = rotate(rms_scale(queries, 1.0), positions[:, None]).astype(jnp.bfloat16)
    fresh_key = rotate(rms_scale(fresh_key, 1.0), positions).astype(jnp.bfloat16)
    return (queries, fresh_key, fresh_value)


def pool_pages(page_table, lengths_here, pool_size, page_len):
    requests_here, max_pages = page_table.shape
    counts = (lengths_here + page_len - 1) // page_len
    matched = (page_table[:, :, None] == jnp.arange(pool_size)[None, None, :]) & (
        jnp.arange(max_pages)[None, :, None] < counts[:, None, None]
    )
    owned_by = jnp.any(matched, axis=1)
    in_use = jnp.any(owned_by, axis=0)
    owners = jnp.sum(
        owned_by.astype(jnp.int32) * jnp.arange(requests_here, dtype=jnp.int32)[:, None], axis=0
    )
    page_pos = jnp.sum(
        matched.astype(jnp.int32) * jnp.arange(max_pages, dtype=jnp.int32)[None, :, None],
        axis=(0, 1),
    )
    return (owners, page_pos, in_use)


def attend(queries, key_self, value_self, page_sets, lengths_here):
    head_size = queries.shape[-1]
    scale_factor = 1.0 / math.sqrt(head_size)
    requests_here = queries.shape[0]
    self_score = (
        jnp.einsum("rgh,rh->rg", queries, key_self, preferred_element_type=jnp.float32)
        * scale_factor
    )
    best_score = self_score
    prepared = []
    for page_keys, page_values, owners, page_pos, in_use in page_sets:
        page_len = page_keys.shape[1]
        member = (owners[:, None] == jnp.arange(requests_here)[None, :]) & in_use[:, None]
        page_queries = jnp.take(queries, owners, axis=0)
        scores = (
            jnp.einsum("pgh,pth->pgt", page_queries, page_keys, preferred_element_type=jnp.float32)
            * scale_factor
        )
        position = page_pos[:, None] * page_len + jnp.arange(page_len)[None, :]
        usable = (position < jnp.take(lengths_here, owners)[:, None]) & in_use[:, None]
        page_best = jnp.max(jnp.where(usable[:, None, :], scores, -jnp.inf), axis=2)
        best_score = jnp.maximum(
            best_score,
            jnp.max(jnp.where(member[:, :, None], page_best[:, None, :], -jnp.inf), axis=0),
        )
        prepared.append((scores, usable, member, owners, page_values))
    self_weight = jnp.exp(self_score - best_score)
    rounded_self = lax.optimization_barrier(self_weight.astype(jnp.bfloat16)).astype(jnp.float32)
    denominator = self_weight
    summed = rounded_self[:, :, None] * value_self.astype(jnp.float32)[:, None, :]
    for scores, usable, member, owners, page_values in prepared:
        shifted = scores - jnp.take(best_score, owners, axis=0)[:, :, None]
        weights = jnp.where(usable[:, None, :], jnp.exp(jnp.minimum(shifted, 0.0)), 0.0)
        selector = member.astype(jnp.float32)
        denominator = denominator + jnp.dot(
            selector.T, jnp.sum(weights, axis=2), precision=lax.Precision.HIGHEST
        )
        page_out = jnp.einsum(
            "pgt,pth->pgh",
            weights.astype(jnp.bfloat16),
            page_values,
            preferred_element_type=jnp.float32,
        )
        summed = summed + jnp.dot(
            selector.T, page_out.reshape(page_out.shape[0], -1), precision=lax.Precision.HIGHEST
        ).reshape(summed.shape)
    return (summed / denominator[:, :, None]).reshape(requests_here, -1).astype(jnp.bfloat16)


def body(
    tokens,
    lengths,
    page_table,
    key_cache,
    value_page_cache,
    mig_slot,
    attn_gain,
    w_query,
    key_weight,
    value_weight,
    w_out,
    moe_gain,
    routes,
    gate_probs,
    w_gate,
    w_up,
    w_down,
):
    req_count = lax.axis_size("req")
    kv_count = lax.axis_size("kv")
    req_here = lax.axis_index("req")
    kv_here = lax.axis_index("kv")
    requests_here, model_width = tokens.shape
    pool_size = key_cache.shape[0]
    page_len = key_cache.shape[2]
    max_pages = page_table.shape[1]
    migrants = mig_slot.shape[1]
    max_len = max_pages * page_len
    partner = (req_here + req_count // 2) % req_count
    own_lengths = lax.dynamic_slice_in_dim(lengths, req_here * requests_here, requests_here)
    own_slots = lax.dynamic_index_in_dim(mig_slot, req_here, 0, keepdims=False)
    partner_slots = lax.dynamic_index_in_dim(mig_slot, partner, 0, keepdims=False)
    partner_lengths = jnp.take(
        lax.dynamic_slice_in_dim(lengths, partner * requests_here, requests_here), partner_slots
    )
    post_lengths = own_lengths.at[own_slots].set(partner_lengths)
    pool_keys = key_cache[:, 0]
    pool_values = value_page_cache[:, 0]
    owners, page_pos, in_use = pool_pages(page_table, own_lengths, pool_size, page_len)
    depart_pages = jnp.take(page_table, own_slots, axis=0)
    depart_mask = jnp.arange(max_len)[None, :] < jnp.take(own_lengths, own_slots)[:, None]
    depart_keys = jnp.where(
        depart_mask[:, :, None],
        jnp.take(pool_keys, depart_pages, axis=0).reshape(migrants, max_len, -1),
        jnp.zeros((), jnp.bfloat16),
    )
    depart_values = jnp.where(
        depart_mask[:, :, None],
        jnp.take(pool_values, depart_pages, axis=0).reshape(migrants, max_len, -1),
        jnp.zeros((), jnp.bfloat16),
    )
    leaving_tokens = jnp.take(tokens, own_slots, axis=0)
    arrived_keys, arrived_values, arrived_tokens = from_behind(
        (depart_keys, depart_values, leaving_tokens), "req", req_count // 2
    )
    settled_tokens = tokens.at[own_slots].set(arrived_tokens)
    queries, fresh_key, fresh_value = project(
        settled_tokens, attn_gain, w_query, key_weight, value_weight, post_lengths
    )
    staying = in_use & jnp.logical_not(jnp.any(owners[:, None] == own_slots[None, :], axis=1))
    arrival_set = (
        arrived_keys.reshape(migrants * max_pages, page_len, -1),
        arrived_values.reshape(migrants * max_pages, page_len, -1),
        jnp.repeat(own_slots, max_pages),
        jnp.tile(jnp.arange(max_pages, dtype=jnp.int32), migrants),
        jnp.ones((migrants * max_pages,), jnp.bool_),
    )
    attended = attend(
        queries,
        fresh_key,
        fresh_value,
        [(pool_keys, pool_values, owners, page_pos, staying), arrival_set],
        post_lengths,
    )
    disp_rows = requests_here // kv_count
    totals = lax.psum(
        jnp.dot(attended, w_out, preferred_element_type=jnp.float32).astype(jnp.bfloat16), "kv"
    ).astype(jnp.float32)
    projected = lax.dynamic_slice_in_dim(totals, kv_here * disp_rows, disp_rows)
    residual_rows = lax.dynamic_slice_in_dim(settled_tokens, kv_here * disp_rows, disp_rows).astype(
        jnp.float32
    )
    hidden = (residual_rows + projected).astype(jnp.bfloat16)
    moe_in = rms_scale(hidden.astype(jnp.float32), moe_gain).astype(jnp.bfloat16)
    devices = req_count * kv_count
    local_experts = w_gate.shape[0]
    expert_total = devices * local_experts
    top_count = routes.shape[1]
    capacity = max(2, 2 * disp_rows * top_count // expert_total)
    flat_routes = routes.reshape(-1)
    expert_hot = (
        flat_routes[:, None] == jnp.arange(expert_total, dtype=jnp.int32)[None, :]
    ).astype(jnp.int32)
    ranking = jnp.sum((jnp.cumsum(expert_hot, axis=0) - expert_hot) * expert_hot, axis=1)
    slot_index = flat_routes * capacity + ranking
    placement = (
        jnp.arange(expert_total * capacity, dtype=jnp.int32)[:, None] == slot_index[None, :]
    ).reshape(expert_total * capacity, disp_rows, top_count)
    placement = jnp.any(placement, axis=2).astype(jnp.bfloat16)
    outgoing = jnp.dot(placement, moe_in, preferred_element_type=jnp.float32).astype(jnp.bfloat16)
    outgoing = outgoing.reshape(devices, local_experts, capacity, model_width)
    received = lax.all_to_all(outgoing, ("req", "kv"), split_axis=0, concat_axis=0, tiled=True)
    gate_part = jnp.einsum("sexd,edf->sexf", received, w_gate, preferred_element_type=jnp.float32)
    up_part = jnp.einsum("sexd,edf->sexf", received, w_up, preferred_element_type=jnp.float32)
    activated = (jax.nn.silu(gate_part) * up_part).astype(jnp.bfloat16)
    returned = lax.all_to_all(
        jnp.einsum("sexf,efd->sexd", activated, w_down, preferred_element_type=jnp.float32).astype(
            jnp.bfloat16
        ),
        ("req", "kv"),
        split_axis=0,
        concat_axis=0,
        tiled=True,
    )
    picked = jnp.take(returned.reshape(-1, model_width), slot_index, axis=0).reshape(
        disp_rows, top_count, model_width
    )
    shares = gate_probs / jnp.sum(gate_probs, axis=1, keepdims=True)
    mixed_rows = hidden.astype(jnp.float32) + jnp.sum(
        shares[:, :, None] * picked.astype(jnp.float32), axis=1
    )
    return (mixed_rows.astype(jnp.bfloat16), arrived_keys[:, None], arrived_values[:, None])


def solution(mesh):
    in_specs = (
        P("req", None),
        P(),
        P("req", None),
        P("req", "kv", None, None),
        P("req", "kv", None, None),
        P(),
        P(),
        P(None, "kv"),
        P(None, "kv"),
        P(None, "kv"),
        P("kv", None),
        P(),
        P(("req", "kv"), None),
        P(("req", "kv"), None),
        P(("req", "kv"), None, None),
        P(("req", "kv"), None, None),
        P(("req", "kv"), None, None),
    )
    out_specs = (P(("req", "kv"), None), P("req", "kv", None, None), P("req", "kv", None, None))
    return jax.shard_map(body, mesh=mesh, in_specs=in_specs, out_specs=out_specs, check_vma=False)
```

profile of v0, /device:TPU:1, one launch (start us, length us, event | category | flops | bytes accessed | tf_op | source)
XLA Modules:
  0.0 262.2 jit_solution(586046590555309745)
XLA Ops:
  7.2 2.0 copy.167
  9.3 1.0 dynamic-slice_reduce_fusion
  10.3 0.8 and_select_fusion.1
  11.1 0.6 gather_fusion.10
  11.7 1.7 gather_fusion
  13.5 3.8 %collective-permute-start = (bf16[2,2048]{1,0:T(2,128)(2,1)S(1)}, bf16[2,2048]{1,0:T(2,128)(2,1)S(1)}, u32[]{:S(2)}, u32[]{:S(2)}) collective-permute-start(bf16[2,2048]{1,0:T(2,128)(2,1)S(1)} %broadcast_select_fusion.3), channel_id=1, source_target_pairs={{0,64},{4,68},{8,72},{12,76},{16,80},{20,84},{24,88},{28,92},{32,9... | collective-permute-start | bytes 24584 | tf_op jit(solution)/shard_map/ppermute | solution.py:13
  17.3 0.8 copy.105
  18.1 0.6 gather_fusion.5
  18.8 4.1 %gather_fusion.12 = bf16[32,64,128]{2,1,0:T(8,128)(2,1)} fusion(bf16[368,64,128]{2,1,0:T(8,128)(2,1)} %bitcast.173, s32[1024]{0:T(1024)S(1)} %pad_clamp_fusion.1), kind=kCustom, calls=%fused_computation.3.clone | custom fusion | bytes 1048704 | tf_op jit(solution)/shard_map/jit(_take)/gather | solution.py:167
  22.9 4.1 %gather_fusion.11 = bf16[32,64,128]{2,1,0:T(8,128)(2,1)} fusion(bf16[368,64,128]{2,1,0:T(8,128)(2,1)} %bitcast.172, s32[1024]{0:T(1024)S(1)} %pad_clamp_fusion.1), kind=kCustom, calls=%fused_computation.1.clone | custom fusion | bytes 1048704 | tf_op jit(solution)/shard_map/jit(_take)/gather | solution.py:162
  27.1 1.4 broadcast_select_fusion
  28.5 1.3 bitcast_select_fusion.1
  29.9 3.0 %collective-permute-start.2 = (bf16[2,1024,128]{2,1,0:T(8,128)(2,1)}, bf16[2,1024,128]{2,1,0:T(8,128)(2,1)}, u32[]{:S(2)}, u32[]{:S(2)}) collective-permute-start(bf16[2,1024,128]{2,1,0:T(8,128)(2,1)} %get-tuple-element.32), channel_id=1, source_target_pairs={{0,64},{4,68},{8,72},{12,76},{16,80},{20,84},{24,88},{28,92},{32,9... | collective-permute-start | bytes 1572872 | tf_op jit(solution)/shard_map/ppermute | solution.py:13
  33.6 0.7 select_reduce_fusion
  34.5 0.6 gather_fusion.9
  35.1 0.6 scatter_fusion.1
  35.8 2.7 %gather_fusion.1 = s32[368]{0:T(512)S(1)} fusion(s32[128]{0:T(128)S(1)} %scatter_fusion.1, s32[1024]{0:T(1024)S(1)} %pad_clamp_fusion.4), kind=kCustom, calls=%fused_computation.5 | custom fusion | bytes 4416 | tf_op jit(solution)/shard_map/jit(_take)/gather | solution.py:88
  39.0 0.8 fusion.64
  39.8 0.7 gather_fusion.3
  40.5 0.7 iota_compare_fusion.4
  42.3 0.6 copy-done.7
  43.3 2.5 scatter_fusion
  45.8 1.2 fusion.47
  47.1 3.1 %convolution_bitcast_fusion = f32[16,8,8,128]{3,1,2,0:T(8,128)S(1)} fusion(bf16[2048,1024]{1,0:T(8,128)(2,1)} %param.28, bf16[128,2048]{1,0:T(8,128)(2,1)} %scatter_fusion, f32[2048]{0:T(1024)S(1)} %copy-done.19, f32[128]{0:T(128)S(1)} %add_rsqrt_fusion.3), kind=kOutput, calls=%fused_computation.55 | convolution fusion | flops 537919488 | bytes 5251584 | tf_op jit(solution)/shard_map/dot_general | solution.py:39
  50.3 0.8 copy-done.2
  51.5 2.0 broadcast_multiply_fusion
  53.6 1.6 multiply_reduce_fusion.3
  55.7 1.4 subtract_convert_fusion
  57.2 0.9 multiply_reduce_fusion.1
  58.1 2.5 gather_fusion.2
  60.6 0.7 gather_fusion.4
  61.3 0.9 copy.124
  62.2 1.6 fusion.42
  63.8 0.7 copy.106
  64.5 7.4 %select_reduce_fusion.2 = (f32[368,8]{1,0:T(8,128)S(1)}, f32[368,8,64]{2,1,0:T(8,128)}) fusion(pred[368,64]{1,0:T(8,128)(4,1)S(1)} %fusion.65, bf16[368,1,64,128]{3,2,1,0:T(8,128)(2,1)} %param.24, bf16[368,8,128]{2,1,0:T(8,128)(2,1)} %gather_fusion.2, pred[368]{0:T(512)(128)(4,1)} %get-tuple-element.18), kind=kOutput, calls=%fused_computation.48 | convolution fusion | flops 49173632 | bytes 7572336 | tf_op jit(solution)/shard_map/pgh,pth->pgt/dot_general | solution.py:84
  72.4 1.6 select_reduce_fusion.5
  74.1 0.6 fusion.91
  75.3 1.3 gather_fusion.7
  76.6 1.2 gather_fusion.6
  77.9 0.9 broadcast_select_fusion.4
  78.8 0.7 broadcast_select_fusion.2
  79.5 2.3 fusion.40
  82.1 3.8 %fusion.51 = f32[368,8,128]{2,1,0:T(8,128)S(1)} fusion(f32[368,8,64]{2,1,0:T(8,128)S(1)} %copy-done.1, f32[368,8]{1,0:T(8,128)S(1)} %broadcast_select_fusion.2, pred[368,64]{1,0:T(8,128)(4,1)S(1)} %copy-done.6, bf16[368,1,64,128]{3,2,1,0:T(8,128)(2,1)} %param.25), kind=kOutput, calls=%fused_computation.70 | convolution fusion | flops 48988160 | bytes 8325632 | tf_op jit(solution)/shard_map/pgt,pth->pgh/dot_general | solution.py:106
  85.9 1.3 fusion.78
  88.0 1.6 fusion.35
  89.5 0.6 fusion.39
  90.2 1.5 convolution_convert_fusion.1
  92.5 41.7 %all-reduce.2.cloned.1.call-done = bf16[128,2048]{1,0:T(8,128)(2,1)} async-done(((bf16[128,2048]{1,0:T(8,128)(2,1)}), bf16[128,2048]{1,0:T(8,128)(2,1)}) %all-reduce.2.cloned.1.call-update) | async-done | bytes 524304 | tf_op jit(solution)/shard_map/psum | solution.py:194
  134.2 1.1 fusion.60
  135.3 2.1 convolution_convert_fusion
  137.5 4.1 %reshape.604 = bf16[128,1,4,2048]{3,2,0,1:T(4,128)(2,1)} reshape(bf16[512,2048]{1,0:T(8,128)(2,1)} %convolution_convert_fusion) | data formatting | bytes 4194304 | tf_op jit(solution)/shard_map/reshape | solution.py:219
  141.6 41.6 %all_to_all.10 = bf16[128,1,4,2048]{3,2,1,0:T(4,128)(2,1)S(1)} all-to-all(bf16[128,1,4,2048]{3,2,1,0:T(4,128)(2,1)} %bitcast.171), channel_id=1, replica_groups=mesh['req'=32,'kv'=4] {'req','kv'}, dimensions={0} | all-to-all | bytes 4194304 | tf_op jit(solution)/shard_map/all_to_all | solution.py:220
  183.2 1.3 copy-done.4
  184.5 4.8 %fusion.4 = f32[128,4,768]{2,0,1:T(8,128)} fusion(bf16[1,2048,768]{2,1,0:T(8,128)(2,1)S(1)} %copy-done.32, bf16[128,1,4,2048]{3,2,1,0:T(4,128)(2,1)S(1)} %all_to_all.10), kind=kOutput, calls=%fused_computation.19 | convolution fusion | flops 1610612736 | bytes 6815744 | tf_op jit(solution)/shard_map/sexd,edf->sexf/dot_general | solution.py:221
  189.3 9.9 %fusion.12 = bf16[128,1,4,2048]{3,0,2,1:T(8,128)(2,1)} fusion(bf16[1,768,2048]{2,1,0:T(8,128)(2,1)S(1)} %copy-done, bf16[1,2048,768]{2,1,0:T(8,128)(2,1)} %param.36, bf16[128,1,4,2048]{3,2,1,0:T(4,128)(2,1)} %copy-done.4, f32[128,4,768]{2,0,1:T(8,128)} %fusion.4), kind=kOutput, calls=%fused_computation.28 | convolution fusion | flops 3224633344 | bytes 12058624 | tf_op jit(solution)/shard_map/sexf,efd->sexd/dot_general | solution.py:225
  199.2 4.5 %copy.119 = bf16[128,1,4,2048]{3,2,1,0:T(4,128)(2,1)} copy(bf16[128,1,4,2048]{3,0,2,1:T(8,128)(2,1)} %fusion.12) | data formatting | bytes 4194304 | tf_op jit(solution)/shard_map/convert_element_type | solution.py:225
  203.7 5.1 %all-to-all-start.1 = ((bf16[128,1,4,2048]{3,2,1,0:T(4,128)(2,1)}), bf16[128,1,4,2048]{3,2,1,0:T(4,128)(2,1)}, u32[]{:S(2)}, u32[]{:S(2)}) async-start(bf16[128,1,4,2048]{3,2,1,0:T(4,128)(2,1)} %copy.119), calls=%async_computation.1 | async-start | bytes 4194304 | tf_op jit(solution)/shard_map/all_to_all | solution.py:224
  209.0 29.8 %all-to-all-done.1 = bf16[128,1,4,2048]{3,2,1,0:T(4,128)(2,1)} async-done(((bf16[128,1,4,2048]{3,2,1,0:T(4,128)(2,1)}), bf16[128,1,4,2048]{3,2,1,0:T(4,128)(2,1)}, u32[]{:S(2)}, u32[]{:S(2)}) %all-to-all-start.1) | async-done | bytes 2097184 | tf_op jit(solution)/shard_map/all_to_all | solution.py:224
  238.9 4.0 %reshape.610 = bf16[512,2048]{1,0:T(8,128)(2,1)} reshape(bf16[128,1,4,2048]{3,2,1,0:T(4,128)(2,1)} %all-to-all-done.1) | data formatting | bytes 4194304 | tf_op jit(solution)/shard_map/reshape | solution.py:233
  242.8 5.2 %gather_fusion.8 = bf16[256,2048]{1,0:T(8,128)(2,1)} fusion(bf16[512,2048]{1,0:T(8,128)(2,1)} %reshape.610, s32[1024]{0:T(1024)S(1)} %pad_clamp_fusion), kind=kCustom, calls=%fused_computation.12 | custom fusion | bytes 2098176 | tf_op jit(solution)/shard_map/jit(_take)/gather | solution.py:233
  248.0 2.9 %multiply_reduce_fusion = f32[32,2048]{1,0:T(8,128)S(1)} fusion(bf16[256,2048]{1,0:T(8,128)(2,1)} %gather_fusion.8, f32[32,8]{1,0:T(8,128)S(1)} %copy.111, pred[32,8]{1,0:T(8,128)(4,1)S(1)} %get-tuple-element.9), kind=kLoop, calls=%fused_computation.32 | loop fusion | flops 2031616 | bytes 1312000 | tf_op jit(solution)/shard_map/reduce_sum | solution.py:237
  250.9 0.7 fusion.63
  251.6 1.9 copy.168
  253.5 1.9 copy.169
  (146 shorter events, 7.4 us)
Async XLA Ops:
  7.2 182.1 %copy-start = (bf16[1,768,2048]{2,1,0:T(8,128)(2,1)S(1)}, bf16[1,768,2048]{2,1,0:T(8,128)(2,1)}, u32[]{:S(2)}) copy-start(bf16[1,768,2048]{2,1,0:T(8,128)(2,1)} %param.37) | copy-start | bytes 9437188
  7.2 127.0 %all-reduce.2.cloned.1.call-start = ((), (), s32[]{:S(2)}) async-start(), calls=%async_computation.2 | async-start | bytes 1048576 | tf_op jit(solution)/shard_map/psum | solution.py:194
  13.5 29.8 %collective-permute-start = (bf16[2,2048]{1,0:T(2,128)(2,1)S(1)}, bf16[2,2048]{1,0:T(2,128)(2,1)S(1)}, u32[]{:S(2)}, u32[]{:S(2)}) collective-permute-start(bf16[2,2048]{1,0:T(2,128)(2,1)S(1)} %broadcast_select_fusion.3), channel_id=1, source_target_pairs={{0,64},{4,68},{8,72},{12,76},{16,80},{20,84},{24,88},{28,92},{32,9... | collective-permute-start | bytes 24584 | tf_op jit(solution)/shard_map/ppermute | solution.py:13
  27.1 5.7 %copy-start.11 = (s32[128,16]{0,1:T(8,128)S(1)}, s32[128,16]{0,1:T(8,128)}, u32[]{:S(2)}) copy-start(s32[128,16]{0,1:T(8,128)} %param.23) | copy-start | bytes 24580
  29.8 42.6 %collective-permute-start.1 = (bf16[2,1024,128]{2,1,0:T(8,128)(2,1)}, bf16[2,1024,128]{2,1,0:T(8,128)(2,1)}, u32[]{:S(2)}, u32[]{:S(2)}) collective-permute-start(bf16[2,1024,128]{2,1,0:T(8,128)(2,1)} %get-tuple-element.33), channel_id=1, source_target_pairs={{0,64},{4,68},{8,72},{12,76},{16,80},{20,84},{24,88},{28,92},{32,9... | collective-permute-start | bytes 1572872 | tf_op jit(solution)/shard_map/ppermute | solution.py:13
  29.9 56.1 %collective-permute-start.2 = (bf16[2,1024,128]{2,1,0:T(8,128)(2,1)}, bf16[2,1024,128]{2,1,0:T(8,128)(2,1)}, u32[]{:S(2)}, u32[]{:S(2)}) collective-permute-start(bf16[2,1024,128]{2,1,0:T(8,128)(2,1)} %get-tuple-element.32), channel_id=1, source_target_pairs={{0,64},{4,68},{8,72},{12,76},{16,80},{20,84},{24,88},{28,92},{32,9... | collective-permute-start | bytes 1572872 | tf_op jit(solution)/shard_map/ppermute | solution.py:13
  34.5 6.7 %copy-start.28 = (s32[32]{0:T(128)}, s32[32]{0:T(128)S(1)}, u32[]{:S(2)}) copy-start(s32[32]{0:T(128)S(1)} %eq.110) | copy-start | bytes 388
  34.5 7.3 %copy-start.27 = (s32[32,8]{0,1:T(8,128)S(1)}, s32[32,8]{0,1:T(8,128)}, u32[]{:S(2)}) copy-start(s32[32,8]{0,1:T(8,128)} %param.33) | copy-start | bytes 3076
  35.7 11.3 %copy-start.19 = (f32[2048]{0:T(1024)S(1)}, f32[2048]{0:T(1024)}, u32[]{:S(2)}) copy-start(f32[2048]{0:T(1024)} %param.27) | copy-start | bytes 24580
  35.8 22.4 %copy-start.12 = (s32[1024]{0:T(1024)}, s32[1024]{0:T(1024)S(1)}, u32[]{:S(2)}) copy-start(s32[1024]{0:T(1024)S(1)} %pad_clamp_fusion.4) | copy-start | bytes 12292
  39.0 11.2 %copy-start.25 = (pred[368]{0:T(512)(128)(4,1)}, pred[368]{0:T(512)(128)(4,1)S(1)}, u32[]{:S(2)}) copy-start(pred[368]{0:T(512)(128)(4,1)S(1)} %not_and_fusion) | copy-start | bytes 1108
  39.8 1.9 copy-start.22
  42.3 0.7 copy-start.7
  43.2 21.4 %copy-start.5 = (pred[368,64]{1,0:T(8,128)(4,1)}, pred[368,64]{1,0:T(8,128)(4,1)S(1)}, u32[]{:S(2)}) copy-start(pred[368,64]{1,0:T(8,128)(4,1)S(1)} %fusion.65) | copy-start | bytes 70660
  43.3 6.9 %copy-start.24 = (s32[128,3]{0,1:T(4,128)}, s32[128,3]{0,1:T(4,128)S(1)}, u32[]{:S(2)}) copy-start(s32[128,3]{0,1:T(4,128)S(1)} %reduce-window.9) | copy-start | bytes 4612
  47.1 6.5 %copy-start.30 = (f32[128]{0:T(128)}, f32[128]{0:T(128)S(1)}, u32[]{:S(2)}) copy-start(f32[128]{0:T(128)S(1)} %add_rsqrt_fusion.3) | copy-start | bytes 1540
  50.3 0.8 copy-start.2
  55.7 6.5 %copy-start.31 = (f32[128]{0:T(128)S(1)}, f32[128]{0:T(128)}, u32[]{:S(2)}) copy-start(f32[128]{0:T(128)} %copy-done.30) | copy-start | bytes 1540
  62.2 11.9 %copy-start.14 = (f32[128,8]{0,1:T(8,128)}, f32[128,8]{0,1:T(8,128)S(1)}, u32[]{:S(2)}) copy-start(f32[128,8]{0,1:T(8,128)S(1)} %copy.124) | copy-start | bytes 12292
  64.5 7.4 %copy-start.10 = (pred[368,128]{1,0:T(8,128)(4,1)S(1)}, pred[368,128]{1,0:T(8,128)(4,1)}, u32[]{:S(2)}) copy-start(pred[368,128]{1,0:T(8,128)(4,1)} %fusion.64) | copy-start | bytes 141316
  64.5 7.9 %copy-start.23 = (pred[32]{0:T(512)(128)(4,1)S(1)}, pred[32]{0:T(512)(128)(4,1)}, u32[]{:S(2)}) copy-start(pred[32]{0:T(512)(128)(4,1)} %get-tuple-element.20) | copy-start | bytes 100
  64.5 9.5 %copy-start.18 = (pred[32,128]{1,0:T(8,128)(4,1)S(1)}, pred[32,128]{1,0:T(8,128)(4,1)}, u32[]{:S(2)}) copy-start(pred[32,128]{1,0:T(8,128)(4,1)} %iota_compare_fusion.4) | copy-start | bytes 12292
  74.7 0.6 copy-start.16
  77.8 4.2 %copy-start.1 = (f32[368,8,64]{2,1,0:T(8,128)S(1)}, f32[368,8,64]{2,1,0:T(8,128)}, u32[]{:S(2)}) copy-start(f32[368,8,64]{2,1,0:T(8,128)} %get-tuple-element.45) | copy-start | bytes 2260996
  77.9 4.2 %copy-start.6 = (pred[368,64]{1,0:T(8,128)(4,1)S(1)}, pred[368,64]{1,0:T(8,128)(4,1)}, u32[]{:S(2)}) copy-start(pred[368,64]{1,0:T(8,128)(4,1)} %copy-done.5) | copy-start | bytes 70660
  82.0 5.3 %copy-start.15 = (f32[128,8]{0,1:T(8,128)S(1)}, f32[128,8]{0,1:T(8,128)}, u32[]{:S(2)}) copy-start(f32[128,8]{0,1:T(8,128)} %copy-done.14) | copy-start | bytes 12292
  82.0 5.3 %copy-start.17 = (f32[128,8]{0,1:T(8,128)S(1)}, f32[128,8]{0,1:T(8,128)}, u32[]{:S(2)}) copy-start(f32[128,8]{0,1:T(8,128)} %copy-done.16) | copy-start | bytes 12292
  82.0 5.3 %copy-start.26 = (pred[368]{0:T(512)(128)(4,1)S(1)}, pred[368]{0:T(512)(128)(4,1)}, u32[]{:S(2)}) copy-start(pred[368]{0:T(512)(128)(4,1)} %copy-done.25) | copy-start | bytes 1108
  82.1 5.7 %copy-start.21 = (bf16[128,8]{0,1:T(8,128)(2,1)S(1)}, bf16[128,8]{0,1:T(8,128)(2,1)}, u32[]{:S(2)}) copy-start(bf16[128,8]{0,1:T(8,128)(2,1)} %get-tuple-element.13) | copy-start | bytes 6148
  82.1 5.7 %copy-start.29 = (s32[32]{0:T(128)S(1)}, s32[32]{0:T(128)}, u32[]{:S(2)}) copy-start(s32[32]{0:T(128)} %copy-done.28) | copy-start | bytes 388
  82.1 5.9 %copy-start.9 = (f32[128,128]{0,1:T(8,128)S(1)}, f32[128,128]{0,1:T(8,128)}, u32[]{:S(2)}) copy-start(f32[128,128]{0,1:T(8,128)} %copy.106) | copy-start | bytes 196612
  87.8 2.4 copy-start.3
  90.2 1.6 slice-start
  90.2 1.6 copy-start.8
  90.2 45.1 %copy-start.20 = (f32[2048]{0:T(1024)S(1)}, f32[2048]{0:T(1024)}, u32[]{:S(2)}) copy-start(f32[2048]{0:T(1024)} %param.32) | copy-start | bytes 24580
  141.6 42.9 %copy-start.32 = (bf16[1,2048,768]{2,1,0:T(8,128)(2,1)S(1)}, bf16[1,2048,768]{2,1,0:T(8,128)(2,1)}, u32[]{:S(2)}) copy-start(bf16[1,2048,768]{2,1,0:T(8,128)(2,1)} %param.35) | copy-start | bytes 9437188
  183.2 1.3 copy-start.4
  203.7 5.2 %copy-start.13 = (f32[32,8]{0,1:T(8,128)S(1)}, f32[32,8]{0,1:T(8,128)}, u32[]{:S(2)}) copy-start(f32[32,8]{0,1:T(8,128)} %param.34) | copy-start | bytes 3076
  203.7 35.2 %all-to-all-start.1 = ((bf16[128,1,4,2048]{3,2,1,0:T(4,128)(2,1)}), bf16[128,1,4,2048]{3,2,1,0:T(4,128)(2,1)}, u32[]{:S(2)}, u32[]{:S(2)}) async-start(bf16[128,1,4,2048]{3,2,1,0:T(4,128)(2,1)} %copy.119), calls=%async_computation.1 | async-start | bytes 4194304 | tf_op jit(solution)/shard_map/all_to_all | solution.py:224
Sparse Core Ops, SparseCore 0:
  91.9 42.2 all-reduce.1
where the time goes:
time: 263 us; the launch traced here: 262 us
  waiting for transfers between devices  71.6 us (27%)
  local copies, waits for them, and re-layouts  55.9 us (21%)
  matrix products  41.6 us (16%)
  blocking collectives  41.6 us (16%)
  other arithmetic  24.9 us (9%)
  between operations  14.7 us (6%)
  starting transfers between devices  11.9 us (5%)
    psum x1, waiting for transfers between devices, body(): lax.psum(jnp.dot(attended, w_out, preferred_element_type=jnp.float32).ast...  41.7 us
    all_to_all x1, blocking collectives, body(): lax.all_to_all(outgoing, ('req', 'kv'), split_axis=0, concat_axis=0, tile...  41.6 us
    all_to_all x1, waiting for transfers between devices, body(): lax.all_to_all(jnp.einsum('sexf,efd->sexd', activated, w_down, preferred_...  29.8 us
    unnamed x74, local copies, waits for them, and re-layouts  10.2 us
    dot_general x1, matrix products, body(): jnp.einsum('sexf,efd->sexd', activated, w_down, preferred_element_type=jn...  9.86 us
    dot_general x2, matrix products, attend(): jnp.einsum('pgh,pth->pgt', page_queries, page_keys, preferred_element_typ...  8.98 us
    ppermute x3, starting transfers between devices, from_behind(): lax.ppermute(shard, axis, [(i, (i + by) % size) for i in range(size)])  6.78 us
  transfers between devices with their start and end apart: 5, of which 2 were waited for; matrix products, arithmetic and copies ran while one was open for 24% of the time, Pallas kernels for 0%

commit v1 on v0

--- a/solution.py
+++ b/solution.py
@@ -6,6 +6,12 @@
 
 EPSILON = 1e-06
 THETA = 1000000.0
+
+
+def gather_and_add(array, mesh_axis):
+    blocks = lax.all_gather(array, mesh_axis, axis=0, tiled=False)
+    total = blocks.sum(axis=0)
+    return total
 
 
 def from_behind(shard, axis, by):
@@ -191,7 +197,7 @@
         post_lengths,
     )
     disp_rows = requests_here // kv_count
-    totals = lax.psum(
+    totals = gather_and_add(
         jnp.dot(attended, w_out, preferred_element_type=jnp.float32).astype(jnp.bfloat16), "kv"
     ).astype(jnp.float32)
     projected = lax.dynamic_slice_in_dim(totals, kv_here * disp_rows, disp_rows)

time: 263 us -> 251 us (0.954)
  waiting for transfers between devices: 71.6 us -> 60.7 us
  blocking collectives: 41.6 us -> 38.9 us
    psum x1 -> x0, waiting for transfers between devices: 41.7 us -> none  [body(): lax.psum(jnp.dot(attended, w_out, preferred_element_type=jnp.float32).ast...]
    all_gather x0 -> x1, waiting for transfers between devices: none -> 30.8 us  [gather_and_add(): blocks = lax.all_gather(array, mesh_axis, axis=0, tiled=False)]
    reduce_sum x0 -> x1, other arithmetic: none -> 2.92 us  [gather_and_add(): total = blocks.sum(axis=0)]
    all_to_all x1, blocking collectives: 41.6 us -> 38.9 us  [body(): lax.all_to_all(outgoing, ('req', 'kv'), split_axis=0, concat_axis=0, tile...]
    unnamed x74 -> x66, local copies, waits for them, and re-layouts: 10.2 us -> 9.54 us
  transfers between devices with their start and end apart: 5 -> 5, of which waited for: 2 -> 2; matrix products, arithmetic and copies ran while one was open for 24% -> 25% of each run, Pallas kernels for 0% -> 0%
where the time goes in v1:
time: 251 us; the launch traced here: 250 us
  waiting for transfers between devices  60.7 us (24%)
  local copies, waits for them, and re-layouts  54.5 us (22%)
  matrix products  41.6 us (17%)
  blocking collectives  38.9 us (15%)
  other arithmetic  27.3 us (11%)
  between operations  14.7 us (6%)
  starting transfers between devices  11.9 us (5%)
    all_to_all x1, blocking collectives, body(): lax.all_to_all(outgoing, ('req', 'kv'), split_axis=0, concat_axis=0, tile...  38.9 us
    all_gather x1, waiting for transfers between devices, gather_and_add(): blocks = lax.all_gather(array, mesh_axis, axis=0, tiled=False)  30.8 us
    all_to_all x1, waiting for transfers between devices, body(): lax.all_to_all(jnp.einsum('sexf,efd->sexd', activated, w_down, preferred_...  29.8 us
    dot_general x1, matrix products, body(): jnp.einsum('sexf,efd->sexd', activated, w_down, preferred_element_type=jn...  9.86 us
    unnamed x66, local copies, waits for them, and re-layouts  9.54 us
    dot_general x2, matrix products, attend(): jnp.einsum('pgh,pth->pgt', page_queries, page_keys, preferred_element_typ...  8.98 us
    ppermute x3, starting transfers between devices, from_behind(): lax.ppermute(shard, axis, [(i, (i + by) % size) for i in range(size)])  6.78 us
    gather x1, local copies, waits for them, and re-layouts, body(): jnp.take(returned.reshape(-1, model_width), slot_index, axis=0)  5.21 us
  transfers between devices with their start and end apart: 5, of which 2 were waited for; matrix products, arithmetic and copies ran while one was open for 25% of the time, Pallas kernels for 0%

profile of v1, /device:TPU:1, one launch (start us, length us, event | category | flops | bytes accessed | tf_op | source)
XLA Modules:
  0.0 249.6 jit_solution(13943218019710830984)
XLA Ops:
  7.2 2.0 copy.166
  9.3 1.0 dynamic-slice_reduce_fusion
  10.3 0.8 and_select_fusion.1
  11.1 0.6 gather_fusion.10
  11.7 1.7 gather_fusion
  13.5 3.8 %collective-permute-start = (bf16[2,2048]{1,0:T(2,128)(2,1)S(1)}, bf16[2,2048]{1,0:T(2,128)(2,1)S(1)}, u32[]{:S(2)}, u32[]{:S(2)}) collective-permute-start(bf16[2,2048]{1,0:T(2,128)(2,1)S(1)} %broadcast_select_fusion.3), channel_id=1, source_target_pairs={{0,64},{4,68},{8,72},{12,76},{16,80},{20,84},{24,88},{28,92},{32,9... | collective-permute-start | bytes 24584 | tf_op jit(solution)/shard_map/ppermute | solution.py:19
  17.3 0.8 copy.105
  18.8 4.1 %gather_fusion.12 = bf16[32,64,128]{2,1,0:T(8,128)(2,1)} fusion(bf16[368,64,128]{2,1,0:T(8,128)(2,1)} %bitcast.174, s32[1024]{0:T(1024)S(1)} %pad_clamp_fusion.1), kind=kCustom, calls=%fused_computation.3.clone | custom fusion | bytes 1048704 | tf_op jit(solution)/shard_map/jit(_take)/gather | solution.py:173
  22.9 4.1 %gather_fusion.11 = bf16[32,64,128]{2,1,0:T(8,128)(2,1)} fusion(bf16[368,64,128]{2,1,0:T(8,128)(2,1)} %bitcast.173, s32[1024]{0:T(1024)S(1)} %pad_clamp_fusion.1), kind=kCustom, calls=%fused_computation.1.clone | custom fusion | bytes 1048704 | tf_op jit(solution)/shard_map/jit(_take)/gather | solution.py:168
  27.1 1.4 broadcast_select_fusion
  28.5 1.3 bitcast_select_fusion.1
  29.9 3.0 %collective-permute-start.2 = (bf16[2,1024,128]{2,1,0:T(8,128)(2,1)}, bf16[2,1024,128]{2,1,0:T(8,128)(2,1)}, u32[]{:S(2)}, u32[]{:S(2)}) collective-permute-start(bf16[2,1024,128]{2,1,0:T(8,128)(2,1)} %get-tuple-element.32), channel_id=1, source_target_pairs={{0,64},{4,68},{8,72},{12,76},{16,80},{20,84},{24,88},{28,92},{32,9... | collective-permute-start | bytes 1572872 | tf_op jit(solution)/shard_map/ppermute | solution.py:19
  33.6 0.7 select_reduce_fusion
  34.5 0.6 gather_fusion.9
  35.1 0.6 scatter_fusion.1
  35.8 2.7 %gather_fusion.1 = s32[368]{0:T(512)S(1)} fusion(s32[128]{0:T(128)S(1)} %scatter_fusion.1, s32[1024]{0:T(1024)S(1)} %pad_clamp_fusion.4), kind=kCustom, calls=%fused_computation.5 | custom fusion | bytes 4416 | tf_op jit(solution)/shard_map/jit(_take)/gather | solution.py:94
  38.4 0.6 broadcast_select_fusion.5
  39.1 0.8 fusion.64
  39.9 0.7 gather_fusion.3
  40.6 0.6 broadcast_select_fusion.7
  41.6 2.5 %scatter_fusion = bf16[128,2048]{1,0:T(8,128)(2,1)} fusion(bf16[128,2048]{1,0:T(8,128)(2,1)} %copy.166, s32[2]{0:T(128)S(1)} %fusion.92, bf16[2,2048]{1,0:T(2,128)(2,1)S(1)} %collective-permute-done), kind=kCustom, calls=%fused_computation.13 | custom fusion | bytes 24584 | tf_op jit(solution)/shard_map/scatter | solution.py:180
  44.2 1.2 fusion.47
  45.4 3.1 %convolution_bitcast_fusion = f32[16,8,8,128]{3,1,2,0:T(8,128)S(1)} fusion(bf16[2048,1024]{1,0:T(8,128)(2,1)} %param.28, bf16[128,2048]{1,0:T(8,128)(2,1)} %scatter_fusion, f32[2048]{0:T(1024)S(1)} %copy-done.16, f32[128]{0:T(128)S(1)} %add_rsqrt_fusion.3), kind=kOutput, calls=%fused_computation.55 | convolution fusion | flops 537919488 | bytes 5251584 | tf_op jit(solution)/shard_map/dot_general | solution.py:45
  48.7 0.8 copy-done.2
  49.9 2.0 broadcast_multiply_fusion
  51.9 1.6 multiply_reduce_fusion.3
  54.1 1.4 subtract_convert_fusion
  55.5 0.9 multiply_reduce_fusion.1
  56.5 2.5 gather_fusion.2
  58.9 0.6 gather_fusion.4
  59.5 0.9 copy.124
  60.4 1.6 fusion.42
  62.0 0.7 copy.106
  62.7 7.4 %select_reduce_fusion.2 = (f32[368,8]{1,0:T(8,128)S(1)}, f32[368,8,64]{2,1,0:T(8,128)}) fusion(pred[368,64]{1,0:T(8,128)(4,1)S(1)} %fusion.65, bf16[368,1,64,128]{3,2,1,0:T(8,128)(2,1)} %param.24, bf16[368,8,128]{2,1,0:T(8,128)(2,1)} %gather_fusion.2, pred[368]{0:T(512)(128)(4,1)S(1)} %copy-done.21), kind=kOutput, calls=%fused_computation.48 | convolution fusion | flops 49173632 | bytes 7572336 | tf_op jit(solution)/shard_map/pgh,pth->pgt/dot_general | solution.py:90
  70.6 1.6 select_reduce_fusion.5
  72.3 0.6 fusion.91
  73.5 0.7 gather_fusion.7
  74.2 1.2 gather_fusion.6
  75.5 0.9 broadcast_select_fusion.4
  76.3 0.8 broadcast_select_fusion.2
  77.1 2.3 fusion.40
  79.7 3.8 %fusion.51 = f32[368,8,128]{2,1,0:T(8,128)S(1)} fusion(f32[368,8,64]{2,1,0:T(8,128)S(1)} %copy-done.1, f32[368,8]{1,0:T(8,128)S(1)} %broadcast_select_fusion.2, pred[368,64]{1,0:T(8,128)(4,1)S(1)} %copy-done.6, bf16[368,1,64,128]{3,2,1,0:T(8,128)(2,1)} %param.25), kind=kOutput, calls=%fused_computation.70 | convolution fusion | flops 48988160 | bytes 8325632 | tf_op jit(solution)/shard_map/pgt,pth->pgh/dot_general | solution.py:112
  83.5 1.3 fusion.78
  85.6 1.6 fusion.35
  87.1 0.6 fusion.39
  87.8 1.5 convolution_convert_fusion.1
  90.6 30.8 %all-gather.3.cloned.1.call-done = bf16[512,2048]{1,0:T(8,128)(2,1)} async-done(((bf16[128,2048]{1,0:T(8,128)(2,1)}), bf16[512,2048]{1,0:T(8,128)(2,1)}) %all-gather.3.cloned.1.call-update) | async-done | bytes 2097168 | tf_op jit(solution)/shard_map/all_gather | solution.py:12
  121.4 2.9 %reduce_sum.125 = bf16[128,2048]{1,0:T(8,128)(2,1)} reduce(bf16[4,128,2048]{2,1,0:T(8,128)(2,1)} %bitcast.179, bf16[]{:T(256)} %constant.231.clone.1), dimensions={0}, to_apply=%region_16.19 | reduce | flops 786432 | bytes 2621442 | tf_op jit(solution)/shard_map/reduce_sum | solution.py:13
  124.3 1.1 fusion.60
  125.5 2.1 convolution_convert_fusion
  127.6 4.1 %reshape.604 = bf16[128,1,4,2048]{3,2,0,1:T(4,128)(2,1)} reshape(bf16[512,2048]{1,0:T(8,128)(2,1)} %convolution_convert_fusion) | data formatting | bytes 4194304 | tf_op jit(solution)/shard_map/reshape | solution.py:225
  131.7 38.9 %all_to_all.10 = bf16[128,1,4,2048]{3,2,1,0:T(4,128)(2,1)S(1)} all-to-all(bf16[128,1,4,2048]{3,2,1,0:T(4,128)(2,1)} %bitcast.172), channel_id=1, replica_groups=mesh['req'=32,'kv'=4] {'req','kv'}, dimensions={0} | all-to-all | bytes 4194304 | tf_op jit(solution)/shard_map/all_to_all | solution.py:226
  170.6 1.3 copy-done.4
  171.9 4.8 %fusion.4 = f32[128,4,768]{2,0,1:T(8,128)} fusion(bf16[1,2048,768]{2,1,0:T(8,128)(2,1)S(1)} %copy-done.28, bf16[128,1,4,2048]{3,2,1,0:T(4,128)(2,1)S(1)} %all_to_all.10), kind=kOutput, calls=%fused_computation.19 | convolution fusion | flops 1610612736 | bytes 6815744 | tf_op jit(solution)/shard_map/sexd,edf->sexf/dot_general | solution.py:227
  176.7 9.9 %fusion.12 = bf16[128,1,4,2048]{3,0,2,1:T(8,128)(2,1)} fusion(bf16[1,768,2048]{2,1,0:T(8,128)(2,1)S(1)} %copy-done, bf16[1,2048,768]{2,1,0:T(8,128)(2,1)} %param.36, bf16[128,1,4,2048]{3,2,1,0:T(4,128)(2,1)} %copy-done.4, f32[128,4,768]{2,0,1:T(8,128)} %fusion.4), kind=kOutput, calls=%fused_computation.28 | convolution fusion | flops 3224633344 | bytes 12058624 | tf_op jit(solution)/shard_map/sexf,efd->sexd/dot_general | solution.py:231
  186.5 4.5 %copy.119 = bf16[128,1,4,2048]{3,2,1,0:T(4,128)(2,1)} copy(bf16[128,1,4,2048]{3,0,2,1:T(8,128)(2,1)} %fusion.12) | data formatting | bytes 4194304 | tf_op jit(solution)/shard_map/convert_element_type | solution.py:231
  191.0 5.1 %all-to-all-start.1 = ((bf16[128,1,4,2048]{3,2,1,0:T(4,128)(2,1)}), bf16[128,1,4,2048]{3,2,1,0:T(4,128)(2,1)}, u32[]{:S(2)}, u32[]{:S(2)}) async-start(bf16[128,1,4,2048]{3,2,1,0:T(4,128)(2,1)} %copy.119), calls=%async_computation.1 | async-start | bytes 4194304 | tf_op jit(solution)/shard_map/all_to_all | solution.py:230
  196.4 29.8 %all-to-all-done.1 = bf16[128,1,4,2048]{3,2,1,0:T(4,128)(2,1)} async-done(((bf16[128,1,4,2048]{3,2,1,0:T(4,128)(2,1)}), bf16[128,1,4,2048]{3,2,1,0:T(4,128)(2,1)}, u32[]{:S(2)}, u32[]{:S(2)}) %all-to-all-start.1) | async-done | bytes 2097184 | tf_op jit(solution)/shard_map/all_to_all | solution.py:230
  226.2 4.0 %reshape.610 = bf16[512,2048]{1,0:T(8,128)(2,1)} reshape(bf16[128,1,4,2048]{3,2,1,0:T(4,128)(2,1)} %all-to-all-done.1) | data formatting | bytes 4194304 | tf_op jit(solution)/shard_map/reshape | solution.py:239
  230.2 5.2 %gather_fusion.8 = bf16[256,2048]{1,0:T(8,128)(2,1)} fusion(bf16[512,2048]{1,0:T(8,128)(2,1)} %reshape.610, s32[1024]{0:T(1024)S(1)} %pad_clamp_fusion), kind=kCustom, calls=%fused_computation.12 | custom fusion | bytes 2098176 | tf_op jit(solution)/shard_map/jit(_take)/gather | solution.py:239
  235.4 2.9 %multiply_reduce_fusion = f32[32,2048]{1,0:T(8,128)S(1)} fusion(bf16[256,2048]{1,0:T(8,128)(2,1)} %gather_fusion.8, f32[32,8]{1,0:T(8,128)S(1)} %copy.111, pred[32,8]{1,0:T(8,128)(4,1)S(1)} %get-tuple-element.9), kind=kLoop, calls=%fused_computation.32 | loop fusion | flops 2031616 | bytes 1312000 | tf_op jit(solution)/shard_map/reduce_sum | solution.py:243
  238.3 0.7 fusion.63
  239.0 1.9 copy.167
  240.9 1.9 copy.168
  (138 shorter events, 7.0 us)
Async XLA Ops:
  7.2 169.5 %copy-start = (bf16[1,768,2048]{2,1,0:T(8,128)(2,1)S(1)}, bf16[1,768,2048]{2,1,0:T(8,128)(2,1)}, u32[]{:S(2)}) copy-start(bf16[1,768,2048]{2,1,0:T(8,128)(2,1)} %param.37) | copy-start | bytes 9437188
  7.2 114.2 %all-gather.3.cloned.1.call-start = ((), (), s32[]{:S(2)}) async-start(), calls=%async_computation.2 | async-start | bytes 2621440 | tf_op jit(solution)/shard_map/all_gather | solution.py:12
  13.5 28.2 %collective-permute-start = (bf16[2,2048]{1,0:T(2,128)(2,1)S(1)}, bf16[2,2048]{1,0:T(2,128)(2,1)S(1)}, u32[]{:S(2)}, u32[]{:S(2)}) collective-permute-start(bf16[2,2048]{1,0:T(2,128)(2,1)S(1)} %broadcast_select_fusion.3), channel_id=1, source_target_pairs={{0,64},{4,68},{8,72},{12,76},{16,80},{20,84},{24,88},{28,92},{32,9... | collective-permute-start | bytes 24584 | tf_op jit(solution)/shard_map/ppermute | solution.py:19
  27.1 5.7 %copy-start.9 = (s32[128,16]{0,1:T(8,128)S(1)}, s32[128,16]{0,1:T(8,128)}, u32[]{:S(2)}) copy-start(s32[128,16]{0,1:T(8,128)} %param.23) | copy-start | bytes 24580
  29.8 40.8 %collective-permute-start.1 = (bf16[2,1024,128]{2,1,0:T(8,128)(2,1)}, bf16[2,1024,128]{2,1,0:T(8,128)(2,1)}, u32[]{:S(2)}, u32[]{:S(2)}) collective-permute-start(bf16[2,1024,128]{2,1,0:T(8,128)(2,1)} %get-tuple-element.33), channel_id=1, source_target_pairs={{0,64},{4,68},{8,72},{12,76},{16,80},{20,84},{24,88},{28,92},{32,9... | collective-permute-start | bytes 1572872 | tf_op jit(solution)/shard_map/ppermute | solution.py:19
  29.9 53.7 %collective-permute-start.2 = (bf16[2,1024,128]{2,1,0:T(8,128)(2,1)}, bf16[2,1024,128]{2,1,0:T(8,128)(2,1)}, u32[]{:S(2)}, u32[]{:S(2)}) collective-permute-start(bf16[2,1024,128]{2,1,0:T(8,128)(2,1)} %get-tuple-element.32), channel_id=1, source_target_pairs={{0,64},{4,68},{8,72},{12,76},{16,80},{20,84},{24,88},{28,92},{32,9... | collective-permute-start | bytes 1572872 | tf_op jit(solution)/shard_map/ppermute | solution.py:19
  34.5 6.2 %copy-start.25 = (s32[32]{0:T(128)}, s32[32]{0:T(128)S(1)}, u32[]{:S(2)}) copy-start(s32[32]{0:T(128)S(1)} %eq.110) | copy-start | bytes 388
  35.1 10.3 %copy-start.16 = (f32[2048]{0:T(1024)S(1)}, f32[2048]{0:T(1024)}, u32[]{:S(2)}) copy-start(f32[2048]{0:T(1024)} %param.27) | copy-start | bytes 24580
  35.7 20.7 %copy-start.10 = (s32[1024]{0:T(1024)}, s32[1024]{0:T(1024)S(1)}, u32[]{:S(2)}) copy-start(s32[1024]{0:T(1024)S(1)} %pad_clamp_fusion.4) | copy-start | bytes 12292
  39.1 9.5 %copy-start.22 = (pred[368]{0:T(512)(128)(4,1)}, pred[368]{0:T(512)(128)(4,1)S(1)}, u32[]{:S(2)}) copy-start(pred[368]{0:T(512)(128)(4,1)S(1)} %not_and_fusion) | copy-start | bytes 1108
  39.9 19.1 %copy-start.19 = (s32[1024]{0:T(1024)}, s32[1024]{0:T(1024)S(1)}, u32[]{:S(2)}) copy-start(s32[1024]{0:T(1024)S(1)} %pad_clamp_fusion.3) | copy-start | bytes 12292
  41.5 21.2 %copy-start.5 = (pred[368,64]{1,0:T(8,128)(4,1)}, pred[368,64]{1,0:T(8,128)(4,1)S(1)}, u32[]{:S(2)}) copy-start(pred[368,64]{1,0:T(8,128)(4,1)S(1)} %fusion.65) | copy-start | bytes 70660
  45.4 6.5 %copy-start.27 = (f32[128]{0:T(128)}, f32[128]{0:T(128)S(1)}, u32[]{:S(2)}) copy-start(f32[128]{0:T(128)S(1)} %add_rsqrt_fusion.3) | copy-start | bytes 1540
  48.7 0.8 copy-start.2
  55.5 7.2 %copy-start.21 = (pred[368]{0:T(512)(128)(4,1)S(1)}, pred[368]{0:T(512)(128)(4,1)}, u32[]{:S(2)}) copy-start(pred[368]{0:T(512)(128)(4,1)} %get-tuple-element.18) | copy-start | bytes 1108
  60.4 11.9 %copy-start.12 = (f32[128,8]{0,1:T(8,128)}, f32[128,8]{0,1:T(8,128)S(1)}, u32[]{:S(2)}) copy-start(f32[128,8]{0,1:T(8,128)S(1)} %copy.124) | copy-start | bytes 12292
  62.7 7.4 %copy-start.8 = (pred[368,128]{1,0:T(8,128)(4,1)S(1)}, pred[368,128]{1,0:T(8,128)(4,1)}, u32[]{:S(2)}) copy-start(pred[368,128]{1,0:T(8,128)(4,1)} %fusion.64) | copy-start | bytes 141316
  62.7 7.9 %copy-start.20 = (pred[32]{0:T(512)(128)(4,1)S(1)}, pred[32]{0:T(512)(128)(4,1)}, u32[]{:S(2)}) copy-start(pred[32]{0:T(512)(128)(4,1)} %get-tuple-element.20) | copy-start | bytes 100
  72.9 0.6 copy-start.14
  75.4 4.2 %copy-start.1 = (f32[368,8,64]{2,1,0:T(8,128)S(1)}, f32[368,8,64]{2,1,0:T(8,128)}, u32[]{:S(2)}) copy-start(f32[368,8,64]{2,1,0:T(8,128)} %get-tuple-element.45) | copy-start | bytes 2260996
  75.5 4.2 %copy-start.6 = (pred[368,64]{1,0:T(8,128)(4,1)S(1)}, pred[368,64]{1,0:T(8,128)(4,1)}, u32[]{:S(2)}) copy-start(pred[368,64]{1,0:T(8,128)(4,1)} %copy-done.5) | copy-start | bytes 70660
  79.6 5.3 %copy-start.13 = (f32[128,8]{0,1:T(8,128)S(1)}, f32[128,8]{0,1:T(8,128)}, u32[]{:S(2)}) copy-start(f32[128,8]{0,1:T(8,128)} %copy-done.12) | copy-start | bytes 12292
  79.6 5.3 %copy-start.15 = (f32[128,8]{0,1:T(8,128)S(1)}, f32[128,8]{0,1:T(8,128)}, u32[]{:S(2)}) copy-start(f32[128,8]{0,1:T(8,128)} %copy-done.14) | copy-start | bytes 12292
  79.6 5.3 %copy-start.23 = (pred[368]{0:T(512)(128)(4,1)S(1)}, pred[368]{0:T(512)(128)(4,1)}, u32[]{:S(2)}) copy-start(pred[368]{0:T(512)(128)(4,1)} %copy-done.22) | copy-start | bytes 1108
  79.7 5.7 %copy-start.18 = (bf16[128,8]{0,1:T(8,128)(2,1)S(1)}, bf16[128,8]{0,1:T(8,128)(2,1)}, u32[]{:S(2)}) copy-start(bf16[128,8]{0,1:T(8,128)(2,1)} %get-tuple-element.13) | copy-start | bytes 6148
  79.7 5.7 %copy-start.26 = (s32[32]{0:T(128)S(1)}, s32[32]{0:T(128)}, u32[]{:S(2)}) copy-start(s32[32]{0:T(128)} %copy-done.25) | copy-start | bytes 388
  79.7 5.9 %copy-start.7 = (f32[128,128]{0,1:T(8,128)S(1)}, f32[128,128]{0,1:T(8,128)}, u32[]{:S(2)}) copy-start(f32[128,128]{0,1:T(8,128)} %copy.106) | copy-start | bytes 196612
  85.4 2.4 copy-start.3
  87.8 1.6 copy-start.24
  89.4 36.1 %copy-start.17 = (f32[2048]{0:T(1024)S(1)}, f32[2048]{0:T(1024)}, u32[]{:S(2)}) copy-start(f32[2048]{0:T(1024)} %param.32) | copy-start | bytes 24580
  131.7 40.2 %copy-start.28 = (bf16[1,2048,768]{2,1,0:T(8,128)(2,1)S(1)}, bf16[1,2048,768]{2,1,0:T(8,128)(2,1)}, u32[]{:S(2)}) copy-start(bf16[1,2048,768]{2,1,0:T(8,128)(2,1)} %param.35) | copy-start | bytes 9437188
  170.6 1.3 copy-start.4
  191.0 5.2 %copy-start.11 = (f32[32,8]{0,1:T(8,128)S(1)}, f32[32,8]{0,1:T(8,128)}, u32[]{:S(2)}) copy-start(f32[32,8]{0,1:T(8,128)} %param.34) | copy-start | bytes 3076
  191.0 35.2 %all-to-all-start.1 = ((bf16[128,1,4,2048]{3,2,1,0:T(4,128)(2,1)}), bf16[128,1,4,2048]{3,2,1,0:T(4,128)(2,1)}, u32[]{:S(2)}, u32[]{:S(2)}) async-start(bf16[128,1,4,2048]{3,2,1,0:T(4,128)(2,1)} %copy.119), calls=%async_computation.1 | async-start | bytes 4194304 | tf_op jit(solution)/shard_map/all_to_all | solution.py:230
Sparse Core Ops, SparseCore 0:
  89.5 31.9 all-gather.2
